TPU v7x, 256 devices: a whole 4x4x8 slice. The times are simulated.
256 devices in a mesh: row: 32 (over z_hi, y, core), col: 8 (over z_lo, x).
Axes of the slice: x: 4, y: 4, z: 8 (z_hi: 4, z_lo: 2; z = z_hi * 2 + z_lo), core: 2. Of those that a mesh axis runs over, the one named last changes fastest.
Arguments:
- left: float32 [128, 16384], P('col', 'row'), may hold values from -12 to 12
- right: float32 [128, 16384], P('row', 'col'), may hold values from -12 to 12
- w_out: float32 [1024, 128], replicated, may hold values from -0.1875 to 0.1875
- b_out: float32 [128], replicated, may hold values from -3 to 3
- pair_grad: float32 [512, 512, 128], P('row', 'col'), may hold values from -6 to 6
Outputs:
- pair_out: float32 [512, 512, 128], P('row', 'col')
- grad_left: float32 [128, 16384], P('col', 'row')
- grad_right: float32 [128, 16384], P('row', 'col')
- grad_weight: float32 [1024, 128], replicated
- grad_bias: float32 [128], replicated
All inputs are finite; a program needn't handle non-finite values.
Results may differ from a plain program's by a relative error of at most 0.0001.
Values sent between devices are 32-bit elements; how exact they have to be, the bound alone decides.
No kernel may reach another device: no remote copies, remote signals or barrier semaphores. Data moves between devices by JAX's collectives and lax.ppermute only.
A program may use at most 128 MiB of HBM per device.

v0:
```python
import jax
import jax.numpy as jnp
from jax import lax
from jax.sharding import PartitionSpec as P

C = 32
Z = 128
S = 128


def body(left, right, w_out, b_out, pair_grad):
    highest = lax.Precision.HIGHEST
    tile_rows = left.shape[1] // C
    tile_cols = right.shape[1] // C
    residues = tile_rows * lax.axis_size("row")
    weight_cube = w_out.reshape(C, C, Z)
    contract_rows = (((0,), (0,)), ((), ()))
    contract_cols = (((1,), (1,)), ((), ()))
    left_all = lax.all_gather(left, "col", axis=0, tiled=True)
    right_all = lax.all_gather(right, "row", axis=0, tiled=True)
    outer = (
        lax.dot_general(
            left_all,
            right_all,
            contract_rows,
            precision=highest,
            preferred_element_type=jnp.float32,
        )
        / S
    )
    outer_split = outer.reshape(tile_rows, C, tile_cols, C)
    pair_out = jnp.einsum("icje,cez->ijz", outer_split, weight_cube, precision=highest) + b_out
    grad_outer = jnp.einsum("ijz,cez->icje", pair_grad, weight_cube, precision=highest)
    grad_outer = grad_outer.reshape(tile_rows * C, tile_cols * C)
    grad_left = lax.psum_scatter(
        lax.dot_general(
            right_all,
            grad_outer,
            contract_cols,
            precision=highest,
            preferred_element_type=jnp.float32,
        )
        / S,
        "col",
        scatter_dimension=0,
        tiled=True,
    )
    grad_right = lax.psum_scatter(
        jnp.dot(left_all, grad_outer, precision=highest) / S, "row", scatter_dimension=0, tiled=True
    )
    weight_term = jnp.einsum("icje,ijz->cez", outer_split, pair_grad, precision=highest).reshape(
        C * C, Z
    )
    bias_term = jnp.sum(pair_grad, axis=(0, 1))
    grad_weight, grad_bias = lax.psum((weight_term, bias_term), ("row", "col"))
    return (pair_out, grad_left, grad_right, grad_weight / residues, grad_bias / residues)


def solution(mesh):
    placed = (P("col", "row"), P("row", "col"), P(), P(), P("row", "col", None))
    return jax.shard_map(
        body,
        mesh=mesh,
        in_specs=placed,
        out_specs=(P("row", "col", None), P("col", "row"), P("row", "col"), P(), P()),
        check_vma=False,
    )
```

profile of v0, /device:TPU:8, one launch (start us, length us, event | category | flops | bytes accessed | tf_op | source)
XLA Modules:
  0.0 770.1 jit_solution(7213743941106208333)
XLA Ops:
  7.2 0.0 all-reduce.6.cloned.1.call-start
  7.2 29.5 %all_gather.6 = f32[128,512]{1,0:T(8,128)S(1)} all-gather(f32[16,512]{1,0:T(8,128)} %param.5), channel_id=1, replica_groups=mesh['row'=32,'col'=8] {'col'}, dimensions={0}, use_global_device_ids=true | all-gather | bytes 294912 | tf_op jit(solution)/shard_map/all_gather | solution.py:19
  36.8 9.8 %convolution_bitcast_fusion = f32[16,32,64,32]{2,3,0,1:T(8,128)} fusion(f32[32,32,128,1]{2,1,3,0:T(8,128)S(1)} %bitcast.42, f32[16,64,128]{2,1,0:T(8,128)} %param.9), kind=kOutput, calls=%fused_computation.1 | convolution fusion | flops 1610612736 | bytes 5242880 | tf_op jit(solution)/shard_map/ijz,cez->icje/dot_general | solution.py:33
  46.6 12.3 %copy.21 = f32[16,32,64,32]{3,2,1,0:T(8,128)} copy(f32[16,32,64,32]{2,3,0,1:T(8,128)} %convolution_bitcast_fusion) | data formatting | bytes 8388608 | tf_op jit(solution)/shard_map/ijz,cez->icje/transpose | solution.py:33
  58.9 13.5 %reshape.24 = f32[512,2048]{1,0:T(8,128)} reshape(f32[16,32,64,32]{3,2,1,0:T(8,128)} %copy.21) | data formatting | bytes 8388608 | tf_op jit(solution)/shard_map/reshape | solution.py:34
  72.4 9.9 %fusion = f32[128,2048]{0,1:T(8,128)} fusion(f32[512,2048]{1,0:T(8,128)} %reshape.24, f32[128,512]{1,0:T(8,128)S(1)} %all_gather.6), kind=kOutput, calls=%fused_computation.3 | convolution fusion | flops 1610874880 | bytes 5505024 | tf_op jit(solution)/shard_map/dot_general | solution.py:49
  82.2 0.0 all-reduce.6.cloned.1.call-update
  82.3 0.0 all-gather.3.cloned.1.call-start
  82.3 0.7 all-gather.3.cloned.1.call-update
  83.0 0.2 all-reduce.4.cloned.1.call-start
  83.3 0.2 reduce_sum.9
  83.4 0.6 dynamic-slice
  84.7 77.5 %psum.15 = f32[128]{0:T(128)S(1)} all-reduce(f32[128]{0:T(128)S(1)} %reduce_sum.9), channel_id=1, replica_groups=mesh['row'=32,'col'=8] {'row','col'}, use_global_device_ids=true, to_apply=%region_4.0 | all-reduce | flops 128 | bytes 1024 | tf_op jit(solution)/shard_map/psum | solution.py:55
  162.1 0.5 broadcast_multiply_fusion.1
  162.6 205.9 %all-reduce.6.cloned.1.call-done = f32[128,2048]{0,1:T(8,128)} async-done(((f32[128,2048]{0,1:T(8,128)}), f32[128,2048]{0,1:T(8,128)}) %all-reduce.6.cloned.1.call-update) | async-done | bytes 1048592
  368.6 1.6 constant_dynamic-slice_fusion
  370.1 0.9 copy.25
  371.1 55.6 %all-gather.3.cloned.1.call-done = f32[32,4,2048]{2,1,0:T(4,128)} async-done(((f32[1,4,2048]{2,1,0:T(4,128)}), f32[32,4,2048]{2,1,0:T(4,128)}) %all-gather.3.cloned.1.call-update) | async-done | bytes 1048592 | tf_op jit(solution)/shard_map/all_gather | solution.py:20
  426.7 1.6 reshape.26
  428.3 5.0 convolution_multiply_fusion
  433.3 11.4 %reshape.22 = f32[16,32,64,32]{3,2,1,0:T(8,128)} reshape(f32[512,2048]{1,0:T(8,128)} %convolution_multiply_fusion) | data formatting | bytes 8388608 | tf_op jit(solution)/shard_map/reshape | solution.py:31
  444.7 12.7 %copy.33 = f32[32,32,16,64]{3,1,0,2:T(8,128)} copy(f32[32,32,16,64]{1,3,0,2:T(8,128)} %bitcast.44) | data formatting | bytes 8388608 | tf_op jit(solution)/shard_map/icje,ijz->cez/dot_general | solution.py:51
  457.4 9.9 %convolution_bitcast_fusion.2 = f32[1024,128]{1,0:T(8,128)} fusion(f32[1024,16,64]{2,0,1:T(8,128)} %bitcast.45, f32[16,64,128]{2,1,0:T(8,128)S(1)} %copy-done.1), kind=kOutput, calls=%fused_computation.5 | convolution fusion | flops 1610612736 | bytes 5242880 | tf_op jit(solution)/shard_map/icje,ijz->cez/dot_general | solution.py:51
  467.3 0.0 all-reduce.4.cloned.1.call-update
  467.3 0.3 reduce-scatter.5.cloned.1.call-start
  467.6 5.2 fusion.2
  472.8 0.8 copy.29
  473.7 0.0 reduce-scatter.5.cloned.1.call-update
  473.7 17.6 %fusion.1 = f32[16,64,128]{2,1,0:T(8,128)} fusion(f32[16,32,64,32]{3,2,1,0:T(8,128)} %reshape.22, f32[32,32,128,1]{2,1,0,3:T(8,128)S(1)} %bitcast.43, f32[128]{0:T(128)S(1)} %copy-done.2), kind=kOutput, calls=%fused_computation.6 | convolution fusion | flops 1610743808 | bytes 5243392 | tf_op jit(solution)/shard_map/icje,cez->ijz/dot_general | solution.py:32
  491.3 230.2 %all-reduce.4.cloned.1.call-done = f32[1024,128]{1,0:T(8,128)} async-done(((f32[1024,128]{1,0:T(8,128)}), f32[1024,128]{1,0:T(8,128)}) %all-reduce.4.cloned.1.call-update) | async-done | bytes 524304 | tf_op jit(solution)/shard_map/psum | solution.py:55
  721.5 1.9 broadcast_multiply_fusion
  723.4 40.2 %reduce-scatter.5.cloned.1.call-done = f32[16,512]{1,0:T(8,128)} async-done(((f32[128,512]{1,0:T(8,128)}), f32[16,512]{1,0:T(8,128)}) %reduce-scatter.5.cloned.1.call-update) | async-done | bytes 32784
  (8 shorter events, 0.0 us)
Async XLA Ops:
  7.2 29.6 %copy-start = (f32[1024,128]{1,0:T(8,128)S(1)}, f32[1024,128]{1,0:T(8,128)}, u32[]{:S(2)}) copy-start(f32[1024,128]{1,0:T(8,128)} %param.7) | copy-start | bytes 1572868
  7.2 361.4 %all-reduce.6.cloned.1.call-start = ((), (), s32[]{:S(2)}) async-start(), calls=%async_computation.4 | async-start | bytes 2097152
  58.9 24.3 %copy-start.1 = (f32[16,64,128]{2,1,0:T(8,128)S(1)}, f32[16,64,128]{2,1,0:T(8,128)}, u32[]{:S(2)}) copy-start(f32[16,64,128]{2,1,0:T(8,128)} %param.9) | copy-start | bytes 1572868
  58.9 24.5 %copy-start.3 = (u32[256]{0:T(256)S(1)}, u32[256]{0:T(256)}, u32[]{:S(2)}) copy-start(u32[256]{0:T(256)} %constant.18) | copy-start | bytes 3076
  82.3 344.4 %all-gather.3.cloned.1.call-start = ((), (), s32[]{:S(2)}) async-start(), calls=%async_computation.2 | async-start | bytes 1081344 | tf_op jit(solution)/shard_map/all_gather | solution.py:20
  83.0 638.5 %all-reduce.4.cloned.1.call-start = ((), (), s32[]{:S(2)}) async-start(), calls=%async_computation.1 | async-start | bytes 1048576 | tf_op jit(solution)/shard_map/psum | solution.py:55
  457.4 16.3 %copy-start.2 = (f32[128]{0:T(128)S(1)}, f32[128]{0:T(128)}, u32[]{:S(2)}) copy-start(f32[128]{0:T(128)} %param.8) | copy-start | bytes 1540
  467.3 296.3 %reduce-scatter.5.cloned.1.call-start = ((), (), s32[]{:S(2)}) async-start(), calls=%async_computation.3 | async-start | bytes 294912
Sparse Core Ops, SparseCore 0:
  82.4 286.1 all-reduce.5
  371.1 55.5 all-gather.2
  467.4 254.0 all-reduce.3
  724.4 39.1 reduce-scatter.4
where the time goes:
time: 771 us; the launch traced here: 770 us
  waiting for transfers between devices  533 us (69%)
  blocking collectives  107 us (14%)
  matrix products  57.4 us (7%)
  local copies, waits for them, and re-layouts  55.4 us (7%)
  between operations  14.5 us (2%)
    unnamed x6, waiting for transfers between devices  247 us
    psum x1, waiting for transfers between devices, body(): grad_weight, grad_bias = lax.psum((weight_term, bias_term), ('row', 'col'))  230 us
    psum x1, blocking collectives, body(): grad_weight, grad_bias = lax.psum((weight_term, bias_term), ('row', 'col'))  77.5 us
    all_gather x1, waiting for transfers between devices, body(): right_all = lax.all_gather(right, 'row', axis=0, tiled=True)  55.6 us
    all_gather x1, blocking collectives, body(): left_all = lax.all_gather(left, 'col', axis=0, tiled=True)  29.5 us
    dot_general x1, matrix products, body(): jnp.einsum('icje,cez->ijz', outer_split, weight_cube, precision=highest)  17.6 us
  transfers between devices with their start and end apart: 4, of which 4 were waited for; matrix products, arithmetic and copies ran while one was open for 4% of the time, Pallas kernels for 0%

commit v1 on v0

--- a/solution.py
+++ b/solution.py
@@ -52,7 +52,7 @@
         C * C, Z
     )
     bias_term = jnp.sum(pair_grad, axis=(0, 1))
-    grad_weight, grad_bias = lax.psum((weight_term, bias_term), ("row", "col"))
+    grad_weight, grad_bias = lax.psum(lax.psum((weight_term, bias_term), "col"), "row")
     return (pair_out, grad_left, grad_right, grad_weight / residues, grad_bias / residues)
 
 

time: 771 us -> 528 us (0.68)
  waiting for transfers between devices: 533 us -> 286 us
    psum x1, waiting for transfers between devices: 230 us -> 34.3 us  [body(): lax.psum((weight_term, bias_term), 'col')]
    all_gather x1, waiting for transfers between devices: 55.6 us -> 26.8 us  [body(): right_all = lax.all_gather(right, 'row', axis=0, tiled=True)]
    unnamed x6, waiting for transfers between devices: 247 us -> 225 us
    psum x1 -> x2, blocking collectives: 77.5 us -> 82.1 us  [the longest x1 64.5 us: body(): lax.psum(lax.psum((weight_term, bias_term), 'col'), 'row')]
  transfers between devices with their start and end apart: 4 -> 4, of which waited for: 4 -> 4; matrix products, arithmetic and copies ran while one was open for 4% -> 14% of each run, Pallas kernels for 0% -> 0%
where the time goes in v1:
time: 528 us; the launch traced here: 527 us
  waiting for transfers between devices  286 us (54%)
  blocking collectives  111 us (21%)
  matrix products  56.7 us (11%)
  local copies, waits for them, and re-layouts  55.5 us (11%)
  between operations  14.5 us (3%)
    unnamed x6, waiting for transfers between devices  225 us
    psum x1, blocking collectives, body(): lax.psum(lax.psum((weight_term, bias_term), 'col'), 'row')  64.5 us
    psum x1, waiting for transfers between devices, body(): lax.psum((weight_term, bias_term), 'col')  34.3 us
    all_gather x1, blocking collectives, body(): left_all = lax.all_gather(left, 'col', axis=0, tiled=True)  29.4 us
    all_gather x1, waiting for transfers between devices, body(): right_all = lax.all_gather(right, 'row', axis=0, tiled=True)  26.8 us
    dot_general x1, matrix products, body(): jnp.einsum('icje,cez->ijz', outer_split, weight_cube, precision=highest)  17.6 us
    psum x1, blocking collectives, body(): lax.psum((weight_term, bias_term), 'col')  17.5 us
    reshape x1, local copies, waits for them, and re-layouts, body(): grad_outer = grad_outer.reshape(tile_rows * C, tile_cols * C)  13.4 us
  transfers between devices with their start and end apart: 4, of which 4 were waited for; matrix products, arithmetic and copies ran while one was open for 14% of the time, Pallas kernels for 0%

profile of v1, /device:TPU:8, one launch (start us, length us, event | category | flops | bytes accessed | tf_op | source)
XLA Modules:
  0.0 526.8 jit_solution(9706006411387811234)
XLA Ops:
  7.2 0.0 all-gather.3.cloned.1.call-start
  7.2 0.7 all-gather.3.cloned.1.call-update
  7.9 0.0 all-reduce.5.cloned.1.call-start
  8.0 29.4 %all_gather.6 = f32[128,512]{1,0:T(8,128)S(1)} all-gather(f32[16,512]{1,0:T(8,128)} %param.5), channel_id=1, replica_groups=mesh['row'=32,'col'=8] {'col'}, dimensions={0}, use_global_device_ids=true | all-gather | bytes 294912 | tf_op jit(solution)/shard_map/all_gather | solution.py:19
  37.4 26.8 %all-gather.3.cloned.1.call-done = f32[32,4,2048]{2,1,0:T(4,128)} async-done(((f32[1,4,2048]{2,1,0:T(4,128)}), f32[32,4,2048]{2,1,0:T(4,128)}) %all-gather.3.cloned.1.call-update) | async-done | bytes 1048592 | tf_op jit(solution)/shard_map/all_gather | solution.py:20
  64.2 1.6 reshape.26
  65.8 5.1 convolution_multiply_fusion
  70.9 11.4 %reshape.22 = f32[16,32,64,32]{3,2,1,0:T(8,128)} reshape(f32[512,2048]{1,0:T(8,128)} %convolution_multiply_fusion) | data formatting | bytes 8388608 | tf_op jit(solution)/shard_map/reshape | solution.py:31
  82.3 12.8 %copy.33 = f32[32,32,16,64]{3,1,0,2:T(8,128)} copy(f32[32,32,16,64]{1,3,0,2:T(8,128)} %bitcast.44) | data formatting | bytes 8388608 | tf_op jit(solution)/shard_map/icje,ijz->cez/dot_general | solution.py:51
  95.1 9.9 %convolution_bitcast_fusion.2 = f32[1024,128]{1,0:T(8,128)} fusion(f32[1024,16,64]{2,0,1:T(8,128)} %bitcast.45, f32[16,64,128]{2,1,0:T(8,128)S(1)} %copy-done.1), kind=kOutput, calls=%fused_computation.5 | convolution fusion | flops 1610612736 | bytes 5242880 | tf_op jit(solution)/shard_map/icje,ijz->cez/dot_general | solution.py:51
  104.9 0.0 all-reduce.5.cloned.1.call-update
  105.0 0.2 all-reduce.7.cloned.1.call-start
  105.2 9.0 %convolution_bitcast_fusion = f32[16,32,64,32]{2,3,0,1:T(8,128)} fusion(f32[32,32,128,1]{2,1,3,0:T(8,128)S(1)} %bitcast.43, f32[16,64,128]{2,1,0:T(8,128)S(1)} %copy-done.1), kind=kOutput, calls=%fused_computation.1 | convolution fusion | flops 1610612736 | bytes 5242880 | tf_op jit(solution)/shard_map/ijz,cez->icje/dot_general | solution.py:33
  114.2 12.3 %copy.21 = f32[16,32,64,32]{3,2,1,0:T(8,128)} copy(f32[16,32,64,32]{2,3,0,1:T(8,128)} %convolution_bitcast_fusion) | data formatting | bytes 8388608 | tf_op jit(solution)/shard_map/ijz,cez->icje/transpose | solution.py:33
  126.5 13.4 %reshape.24 = f32[512,2048]{1,0:T(8,128)} reshape(f32[16,32,64,32]{3,2,1,0:T(8,128)} %copy.21) | data formatting | bytes 8388608 | tf_op jit(solution)/shard_map/reshape | solution.py:34
  140.0 9.9 %fusion = f32[128,2048]{0,1:T(8,128)} fusion(f32[512,2048]{1,0:T(8,128)} %reshape.24, f32[128,512]{1,0:T(8,128)S(1)} %all_gather.6), kind=kOutput, calls=%fused_computation.3 | convolution fusion | flops 1610874880 | bytes 5505024 | tf_op jit(solution)/shard_map/dot_general | solution.py:49
  149.9 34.3 %all-reduce.5.cloned.1.call-done = f32[1024,128]{1,0:T(8,128)} async-done(((f32[1024,128]{1,0:T(8,128)}), f32[1024,128]{1,0:T(8,128)}) %all-reduce.5.cloned.1.call-update) | async-done | bytes 524304 | tf_op jit(solution)/shard_map/psum | solution.py:55
  184.2 0.0 reduce-scatter.5.cloned.1.call-start
  184.3 0.2 reduce_sum.9
  184.4 0.6 dynamic-slice
  185.7 17.5 %psum.30 = f32[128]{0:T(128)S(1)} all-reduce(f32[128]{0:T(128)S(1)} %reduce_sum.9), channel_id=1, replica_groups=mesh['row'=32,'col'=8] {'col'}, use_global_device_ids=true, to_apply=%region_5.0 | all-reduce | flops 128 | bytes 1024 | tf_op jit(solution)/shard_map/psum | solution.py:55
  203.2 64.5 %psum.31 = f32[128]{0:T(128)S(1)} all-reduce(f32[128]{0:T(128)S(1)} %psum.30), channel_id=1, replica_groups=mesh['row'=32,'col'=8] {'row'}, use_global_device_ids=true, to_apply=%region_6.0 | all-reduce | flops 128 | bytes 1024 | tf_op jit(solution)/shard_map/psum | solution.py:55
  267.7 0.5 broadcast_multiply_fusion.1
  268.3 5.2 fusion.2
  273.5 0.8 copy.29
  274.3 0.0 reduce-scatter.5.cloned.1.call-update
  274.4 17.6 %fusion.1 = f32[16,64,128]{2,1,0:T(8,128)} fusion(f32[16,32,64,32]{3,2,1,0:T(8,128)} %reshape.22, f32[32,32,128,1]{2,1,0,3:T(8,128)S(1)} %bitcast.42, f32[128]{0:T(128)S(1)} %copy-done.2), kind=kOutput, calls=%fused_computation.6 | convolution fusion | flops 1610743808 | bytes 5243392 | tf_op jit(solution)/shard_map/icje,cez->ijz/dot_general | solution.py:32
  291.9 180.5 %all-reduce.7.cloned.1.call-done = (f32[128,2048]{0,1:T(8,128)}, f32[1024,128]{1,0:T(8,128)}) async-done(((f32[128,2048]{0,1:T(8,128)}, f32[1024,128]{1,0:T(8,128)}), (f32[128,2048]{0,1:T(8,128)}, f32[1024,128]{1,0:T(8,128)})) %all-reduce.7.cloned.1.call-update) | async-done | bytes 1572880
  472.4 1.6 constant_dynamic-slice_fusion
  473.9 0.9 copy.25
  474.9 1.9 broadcast_multiply_fusion
  476.8 43.5 %reduce-scatter.5.cloned.1.call-done = f32[16,512]{1,0:T(8,128)} async-done(((f32[128,512]{1,0:T(8,128)}), f32[16,512]{1,0:T(8,128)}) %reduce-scatter.5.cloned.1.call-update) | async-done | bytes 32784
  (9 shorter events, 0.0 us)
Async XLA Ops:
  7.2 98.0 %copy-start = (f32[1024,128]{1,0:T(8,128)S(1)}, f32[1024,128]{1,0:T(8,128)}, u32[]{:S(2)}) copy-start(f32[1024,128]{1,0:T(8,128)} %param.7) | copy-start | bytes 1572868
  7.2 57.0 %all-gather.3.cloned.1.call-start = ((), (), s32[]{:S(2)}) async-start(), calls=%async_computation.2 | async-start | bytes 1081344 | tf_op jit(solution)/shard_map/all_gather | solution.py:20
  7.9 176.3 %all-reduce.5.cloned.1.call-start = ((), (), s32[]{:S(2)}) async-start(), calls=%async_computation.1 | async-start | bytes 1048576 | tf_op jit(solution)/shard_map/psum | solution.py:55
  82.3 12.8 %copy-start.1 = (f32[16,64,128]{2,1,0:T(8,128)S(1)}, f32[16,64,128]{2,1,0:T(8,128)}, u32[]{:S(2)}) copy-start(f32[16,64,128]{2,1,0:T(8,128)} %param.9) | copy-start | bytes 1572868
  105.0 367.4 %all-reduce.7.cloned.1.call-start = ((), (), s32[]{:S(2)}) async-start(), calls=%async_computation.4 | async-start | bytes 3145728
  126.5 57.9 %copy-start.3 = (u32[256]{0:T(256)S(1)}, u32[256]{0:T(256)}, u32[]{:S(2)}) copy-start(u32[256]{0:T(256)} %constant.18) | copy-start | bytes 3076
  140.0 134.4 %copy-start.2 = (f32[128]{0:T(128)S(1)}, f32[128]{0:T(128)}, u32[]{:S(2)}) copy-start(f32[128]{0:T(128)} %param.8) | copy-start | bytes 1540
  184.2 336.0 %reduce-scatter.5.cloned.1.call-start = ((), (), s32[]{:S(2)}) async-start(), calls=%async_computation.3 | async-start | bytes 294912
Sparse Core Ops, SparseCore 0:
  10.5 53.5 all-gather.2
  105.1 79.0 all-reduce.4
  186.9 285.4 all-reduce.6
  475.3 44.8 reduce-scatter.4
